TPU v7x, 32 devices: a whole 2x2x4 slice. The times are simulated.
32 devices in a mesh: dp: 8 (over z, y), mp: 4 (over x, core).
Axes of the slice: x: 2, y: 2, z: 4, core: 2. Of those that a mesh axis runs over, the one named last changes fastest.
Arguments:
- hidden: bfloat16 [16384, 768], P('dp'), may hold values from -6 to 6
- upstream: bfloat16 [16384, 768], P('dp'), may hold values from -3 to 3
- segment_ids: int32 [16384], P('dp'), may hold values from 0 to 16, as said below
- cls_positions: int32 [16, 16], P('dp'), may hold values from 0 to 872, as said below
- positives: int32 [128], replicated, may hold values from 0 to 127, each once
- w_query: bfloat16 [768, 768], P(None, 'mp'), may hold values from -0.21875 to 0.21875
- b_query: float32 [768], P('mp'), may hold values from -3 to 3
- w_key: bfloat16 [768, 768], P(None, 'mp'), may hold values from -0.21875 to 0.21875
- w_value: bfloat16 [768, 768], P(None, 'mp'), may hold values from -0.21875 to 0.21875
- b_value: float32 [768], P('mp'), may hold values from -3 to 3
- w_out: bfloat16 [768, 768], P('mp'), may hold values from -1.25 to 1.25
- b_out: float32 [768], replicated, may hold values from -2.5 to 2.5
- gain_attn: float32 [768], replicated, may hold values from 0.5 to 1.5
- shift_attn: float32 [768], replicated, may hold values from -2.5 to 2.5
- w_inner: bfloat16 [768, 3072], P(None, 'mp'), may hold values from -0.21875 to 0.21875
- b_inner: float32 [3072], P('mp'), may hold values from -3 to 3
- w_outer: bfloat16 [3072, 768], P('mp'), may hold values from -0.109375 to 0.109375
- b_outer: float32 [768], replicated, may hold values from -2.5 to 2.5
- gain_final: float32 [768], replicated, may hold values from 0.5 to 1.5
- shift_final: float32 [768], replicated, may hold values from -2.5 to 2.5
Outputs:
- mean_loss: float32 [1], replicated
- layer_out: bfloat16 [16384, 768], P('dp')
- grad_hidden: float32 [16384, 768], P('dp')
- grad_w_query: float32 [768, 768], P(None, 'mp')
- grad_b_query: float32 [768], P('mp')
- grad_w_key: float32 [768, 768], P(None, 'mp')
- grad_w_value: float32 [768, 768], P(None, 'mp')
- grad_b_value: float32 [768], P('mp')
- grad_w_out: float32 [768, 768], P('mp')
- grad_b_out: float32 [768], replicated
- grad_gain_attn: float32 [768], replicated
- grad_shift_attn: float32 [768], replicated
- grad_w_inner: float32 [768, 3072], P(None, 'mp')
- grad_b_inner: float32 [3072], P('mp')
- grad_w_outer: float32 [3072, 768], P('mp')
- grad_b_outer: float32 [768], replicated
- grad_gain_final: float32 [768], replicated
- grad_shift_final: float32 [768], replicated
Inputs may be any that keep to these rules, and one draw needn't show every extreme that they name: `segment_ids`: each packed row of 1024 tokens holds 16 consecutive segments numbered 0 to 15 in order, even numbers queries and odd numbers passages, then padding tokens numbered 2 * 8, of which every row has some. `cls_positions`: entry j < 8 of row r is the first position within the row of segment 2 j, entry 8 + j that of segment 2 j + 1, as given by segment_ids. `positives`: every passage is the positive of exactly one query.
All inputs are finite; a program needn't handle non-finite values.
Results may differ from a plain program's by a relative error of at most 0.013.
Values may be sent and summed in bfloat16 or wider, within the bound.
A program may use at most 128 MiB of HBM per device.

v0:
```python
from functools import partial
import math

import jax
import jax.numpy as jnp
from jax import lax
from jax.experimental import pallas as pl
from jax.experimental.pallas import tpu as pltpu
from jax.sharding import PartitionSpec as P

D = 768
HEAD_DIM = 64
LEN = 1024
PAIRS = 8
BLOCK = 128
BF16 = jnp.bfloat16
F32 = jnp.float32
MESH = pl.DeviceIdType.MESH
FORWARD_TASKS = (0, 2, 2, 4, 4, 6, 7, 8, 9, 10, 11, 12, 13, 14, 15)
HIGHEST = lax.Precision.HIGHEST
VMEM = pl.BlockSpec(memory_space=pltpu.VMEM)
ANY = pl.BlockSpec(memory_space=pl.ANY)


def dot(left_arr, right_arr, left_dim=1, right_dim=0, precision=None):
    return lax.dot_general(
        left_arr,
        right_arr,
        (((left_dim,), (right_dim,)), ((), ())),
        preferred_element_type=F32,
        precision=precision,
    )


def norm_forward(summed, gain_vec, offset_vec):
    centre = summed - jnp.mean(summed, axis=-1, keepdims=True)
    inverse = lax.rsqrt(jnp.mean(centre * centre, axis=-1, keepdims=True) + 1e-12)
    normed = centre * inverse
    return (normed * gain_vec + offset_vec, normed, inverse)


def norm_backward(grad_rows, normed, inverse, gain_vec):
    scaled = grad_rows * gain_vec
    return inverse * (
        scaled
        - jnp.mean(scaled, axis=-1, keepdims=True)
        - normed * jnp.mean(scaled * normed, axis=-1, keepdims=True)
    )


def as_row(ref):
    return ref[...].reshape(1, -1)


def sum_rows(arr):
    return jnp.sum(arr, axis=0, keepdims=True)


def head_masks(heads, dtype):
    lane = lax.broadcasted_iota(jnp.int32, (1, heads * HEAD_DIM), 1)
    return [
        ((lane >= h * HEAD_DIM) & (lane < (h + 1) * HEAD_DIM)).astype(F32).astype(dtype)
        for h in range(heads)
    ]


def stack_heads(rows, masks):
    return jnp.concatenate([rows * mask for mask in masks], axis=0)


def merge_heads(stacked, masks):
    total = None
    for h, mask in enumerate(masks):
        part = stacked[h * BLOCK : (h + 1) * BLOCK] * mask
        total = part if total is None else total + part
    return total


def masked_soft(scores, same, heads):
    parts = []
    for h in range(heads):
        part = jnp.where(same, scores[h * BLOCK : (h + 1) * BLOCK], -1e30)
        part = jnp.exp(part - jnp.max(part, axis=-1, keepdims=True))
        parts.append(part * (1.0 / jnp.sum(part, axis=-1, keepdims=True)))
    return jnp.concatenate(parts, axis=0)


def same_segment(seg_row, base, keys):
    mine = jnp.broadcast_to(seg_row[:, pl.ds(base, BLOCK)], (BLOCK, BLOCK))
    return jnp.transpose(mine)[:, :1] == seg_row[:, keys]


def remote(src, dst, send, recv, at, device):
    return pltpu.make_async_remote_copy(
        src_ref=src,
        dst_ref=dst,
        send_sem=send.at[at],
        recv_sem=recv.at[at],
        device_id=device,
        device_id_type=MESH,
    )


def greet(devices):
    barrier = pltpu.get_barrier_semaphore()
    for device in devices:
        pl.semaphore_signal(barrier, inc=1, device_id=device, device_id_type=MESH)
    pl.semaphore_wait(barrier, len(devices))


def forward_kernel(
    hidden_ref, wq_ref, bq_ref, wk_ref, wv_ref, bv_ref, seg_ref, wi_ref, wo_ref, wp_ref, bi_ref,
    q_ref, k_ref, v_ref, ctx_ref, wi_all, wo_all, wp_all, bi_all,
    ctx_s, send, recv, local,
):
    dp, me = lax.axis_index("dp"), lax.axis_index("mp")
    tokens = hidden_ref.shape[0]
    own = tokens // 4
    width = q_ref.shape[1]
    heads = width // HEAD_DIM
    core, far, diag = (dp, me ^ 1), (dp, me ^ 2), (dp, me ^ 3)
    sides = ((dp ^ 1, me), (dp ^ 2, me))
    quarter_at = dp % 4

    pieces = []
    for mine, every in ((wp_ref, wp_all), (wi_ref, wi_all), (wo_ref, wo_all)):
        rows = mine.shape[0] // 4
        step = rows if rows < 128 else rows // 2
        for first in range(0, rows, step):
            pieces.append((mine, every, first, step, rows))
    count = len(pieces)

    def rows_of(piece, which):
        first, step, rows = piece[2:]
        return pl.ds(pl.multiple_of(which * rows + first, 16), step)

    x_copies, side_copies, core_copies = [], [], []
    for i, piece in enumerate(pieces):
        mine, every = piece[:2]
        one, two = (0, 1) if i % 2 == 0 else (1, 0)
        at = [
            rows_of(piece, quarter_at ^ bits)
            for bits in (0, 1 << one, 1 << two, 3)
        ]

        def pair(t, to, sem):
            return [
                remote(every.at[2, at[r]], every.at[2, at[r]], send, recv, sem, sides[to])
                for r in t
            ]

        x_copies.append(remote(mine.at[at[0]], every.at[2, at[0]], send, recv, 8 * i, far))
        side_copies.append(
            (
                pair((0, 1), one, 8 * i + 1),
                pair((0, 2), two, 8 * i + 2),
                pair((1, 3), two, 8 * i + 3),
            )
        )
        core_copies.append(
            [
                remote(every.at[2, at[r]], every.at[3, at[r]], send, recv, 8 * i + 4 + r, core)
                for r in range(4)
            ]
        )
    base = 8 * count
    near = []
    for mine, every in ((wp_ref, wp_all), (wi_ref, wi_all), (wo_ref, wo_all)):
        near.append(remote(mine, every.at[1], send, recv, base, core))
        base += 1
    bi_all[0] = bi_ref[...].reshape(1, -1)
    biases = [
        remote(bi_all.at[0], bi_all.at[b], send, recv, base + b - 1, (dp, me ^ b))
        for b in (1, 2, 3)
    ]
    base += 3
    first_row = 1 - me // 2

    def ctx_copy(b):
        block = pl.ds(pl.multiple_of((me ^ b) * own, own), own)
        return remote(ctx_s.at[block], ctx_ref.at[b], send, recv, base + b - 1, (dp, me ^ b))

    greet([core, far, diag, sides[0], sides[1]])
    for copy in x_copies[:2] + near + biases:
        copy.start()
    keeps = [
        pltpu.make_async_copy(mine, every.at[0], local.at[i])
        for i, (mine, every) in enumerate(((wp_ref, wp_all), (wi_ref, wi_all), (wo_ref, wo_all)))
    ]
    for copy in keeps:
        copy.start()

    masks, masks_f = head_masks(heads, BF16), head_masks(heads, F32)

    def project(row):
        at = pl.ds(pl.multiple_of(row * LEN, LEN), LEN)
        rows = hidden_ref[at, :]
        scale = 1.0 / math.sqrt(HEAD_DIM)
        q_ref[at, :] = ((dot(rows, wq_ref[...], 1, 1) + bq_ref[...]) * scale).astype(BF16)
        k_ref[at, :] = dot(rows, wk_ref[...], 1, 1).astype(BF16)
        v_ref[at, :] = (dot(rows, wv_ref[...], 1, 1) + bv_ref[...]).astype(BF16)

    def attend(row, b):
        keys = pl.ds(pl.multiple_of(row * LEN, LEN), LEN)
        at = pl.ds(pl.multiple_of(row * LEN + b * BLOCK, BLOCK), BLOCK)
        q3 = stack_heads(q_ref[at, :], masks)
        scores = dot(q3, k_ref[keys, :], 1, 1)
        same = same_segment(seg_ref.at[row], pl.multiple_of(b * BLOCK, BLOCK), slice(None))
        weights = masked_soft(scores, same, heads).astype(BF16)
        ctx_s[at, :] = merge_heads(dot(weights, v_ref[keys, :]), masks_f).astype(BF16)

    def got_x(i):
        x_copies[i].wait_recv()
        if i + 2 < count:
            x_copies[i + 2].start()
        side_copies[i][0][0].start()
        side_copies[i][1][0].start()
        core_copies[i][0].start()

    def got_one(i):
        side_copies[i][0][1].wait_recv()
        side_copies[i][2][0].start()
        core_copies[i][1].start()

    def got_two(i):
        side_copies[i][1][1].wait_recv()
        core_copies[i][2].start()
        side_copies[i][2][1].wait_recv()
        core_copies[i][3].start()

    todo = []
    for t in range(count + 4):
        for act, lag in ((got_x, 0), (got_one, 1), (got_two, 3)):
            if 0 <= t - lag < count:
                todo.append((act, t - lag))

    to_far = [ctx_copy(2), ctx_copy(3)]
    blocks = LEN // BLOCK

    def send_far(_):
        for copy in to_far:
            copy.start()

    schedule = {}
    for n, task in enumerate(todo):
        schedule.setdefault(FORWARD_TASKS[n], []).append(task)
    schedule.setdefault(blocks - 1, []).append((send_far, 0))

    def row_step(i, carry):
        row = first_row + i * (1 - 2 * first_row)
        project(row)

        def block_step(b, inner):
            attend(row, b)
            for when, tasks in schedule.items():

                @pl.when(i * blocks + b == when)
                def _(tasks=tasks):
                    for act, n in tasks:
                        act(n)

            return inner

        lax.fori_loop(0, blocks, block_step, 0)
        return carry

    lax.fori_loop(0, 2, row_step, 0)
    to_core = ctx_copy(1)
    to_core.start()
    ctx_ref[0] = ctx_s[pl.ds(pl.multiple_of(me * own, own), own), :]
    for copy in keeps:
        copy.wait()
    for copy in near + biases + to_far + [to_core]:
        copy.wait()
    for i in range(count):
        x_copies[i].wait_send()
        for sent, _ in side_copies[i]:
            sent.wait_send()
        for copy in core_copies[i]:
            copy.wait()


def forward_attention(hidden, wq, bq, wk, wv, bv, seg, wi, wo, wp, bi):
    tokens, width, units = hidden.shape[0], wq.shape[0], wi.shape[1]
    shape = jax.ShapeDtypeStruct
    copies = 8 * 5 + 9
    return pl.pallas_call(
        forward_kernel,
        out_shape=[shape((tokens, width), BF16)] * 3
        + [
            shape((4, tokens // 4, width), BF16),
            shape((4, D, units), BF16),
            shape((4, units, D), BF16),
            shape((4, width, D), BF16),
            shape((4, 1, units), F32),
        ],
        in_specs=[VMEM] * 11,
        out_specs=[VMEM] * 4 + [ANY, ANY, ANY, VMEM],
        scratch_shapes=[
            pltpu.VMEM((tokens, width), BF16),
            pltpu.SemaphoreType.DMA((copies,)),
            pltpu.SemaphoreType.DMA((copies,)),
            pltpu.SemaphoreType.DMA((3,)),
        ],
        compiler_params=pltpu.CompilerParams(
            collective_id=0, has_side_effects=True, vmem_limit_bytes=56 << 20
        ),
        cost_estimate=pl.CostEstimate(
            flops=8 * 10**9, bytes_accessed=24 << 20, transcendentals=1 << 22
        ),
        name="forward_attention",
    )(hidden, wq, bq, wk, wv, bv, seg, wi, wo, wp, bi)


def early_rows(units):
    return units * 2 // 3


def add_low(left, right):
    return (left.astype(F32) + right.astype(F32)).astype(BF16)


def loss_part(picked_s, target_ref, loss_ref, got, every, log_s, send, recv, send_all, recv_all, after):
    dp, me = lax.axis_index("dp"), lax.axis_index("mp")
    count = lax.axis_size("dp")
    size = 2 * PAIRS
    side = me % 2
    copies = [remote(picked_s, got.at[b], send, recv, b - 1, (dp, me ^ b)) for b in (1, 2, 3)]
    for copy in copies:
        copy.start()
    got[0] = picked_s[...]
    for copy in copies:
        copy.wait()
    every[side, dp] = add_low(got[(2 * side) ^ me], got[(2 * side + 1) ^ me])

    def peer_copy(d, owner, peer):
        return pltpu.make_async_remote_copy(
            src_ref=every.at[side, owner],
            dst_ref=every.at[side, owner],
            send_sem=send_all.at[d],
            recv_sem=recv_all.at[d],
            device_id=(peer, me),
            device_id_type=MESH,
        )

    def start(d, carry):
        peer_copy(d, dp, lax.rem(dp + d, count)).start()
        return carry

    def finish(d, carry):
        peer = lax.rem(dp + count - d, count)
        peer_copy(d, dp, lax.rem(dp + d, count)).wait_send()
        peer_copy(d, peer, peer).wait_recv()
        return carry

    lax.fori_loop(1, count, start, 0)
    after()
    lax.fori_loop(1, count, finish, 0)
    swap = remote(every.at[side], every.at[side], send, recv, 3, (dp, me ^ 1))
    swap.start()
    swap.wait()

    scale = 3.0 / math.sqrt(D)
    total = count * 2 * size
    part = min(total, 256)
    vecs = every[...].reshape(total, D)
    col_at = lax.broadcasted_iota(jnp.int32, (1, total), 1)
    row_at = lax.broadcasted_iota(jnp.int32, (total, 1), 0)
    passage_row = (row_at & (size - 1)) >= PAIRS
    query_col = (col_at & (size - 1)) < PAIRS
    loss = jnp.zeros((1, 1), F32)
    for low in range(0, total, part):
        cols = slice(low, low + part)
        logits = dot(vecs, vecs[cols], 1, 1) * scale
        masked = jnp.where(passage_row, logits, -1e30)
        largest = jnp.max(masked, axis=0, keepdims=True)
        log_total = largest + jnp.log(jnp.sum(jnp.exp(masked - largest), axis=0, keepdims=True))
        log_s[:, cols] = log_total
        hit = jnp.sum(
            jnp.where(row_at == target_ref[:, cols], logits, 0.0), axis=0, keepdims=True
        )
        cross = jnp.where(query_col[:, cols], log_total - hit, 0.0)
        loss = loss + jnp.sum(cross, axis=1, keepdims=True)
    loss_ref[...] = loss * (1.0 / (total // 2))

    base = (me // 2 * count + dp) * size
    own = every[me // 2, dp]
    own_at = lax.broadcasted_iota(jnp.int32, (size, 1), 0)
    logits = dot(own, vecs, 1, 1) * scale
    masked = jnp.where(query_col, -1e30, logits)
    largest = jnp.max(masked, axis=1, keepdims=True)
    expo = jnp.exp(masked - largest)
    own_soft = expo / jnp.sum(expo, axis=1, keepdims=True)
    all_soft = jnp.exp(jnp.where(query_col, logits - log_s[...], -1e30))
    all_hit = (target_ref[...] == own_at + base).astype(F32)
    own_target = jnp.sum(
        jnp.where(col_at == own_at + base, target_ref[...], 0), axis=1, keepdims=True
    )
    own_hit = (own_target == col_at).astype(F32)
    grad = jnp.where(own_at < PAIRS, own_soft - own_hit, all_soft - all_hit) * scale
    return dot(grad, vecs.astype(F32), precision=HIGHEST)


def middle_kernel(
    ctx_in, wp_in, hidden_in, up_in, wi_in, wo_in, bi_ref, bp_ref, bo_ref, ga_ref, sa_ref, gf_ref,
    sf_ref, spots_ref, target_ref,
    out_ref, one_out, dctx_ref, sum_a, sum_b, far_b, common_ref, loss_ref,
    ctx_s, wp_s, low_s, up_s, wi_s, wo_s, act_s, slope_s, mid_s, n1_s, i1_s, n2_s, i2_s,
    middle_s, sum_s, out_s, wide_s, mine_a, sent_a, got_a, mine_b, sent_b, got_b,
    picked_s, got, every, log_s,
    send, recv, local, send_l, recv_l, send_all, recv_all,
):
    dp, me = lax.axis_index("dp"), lax.axis_index("mp")
    count = lax.axis_size("dp")
    own = n1_s.shape[0]
    units, width = wi_s.shape[2], wp_s.shape[1]
    core, far, diag = (dp, me ^ 1), (dp, me ^ 2), (dp, me ^ 3)
    block = lambda b: pl.ds(pl.multiple_of((me ^ b) * own, own), own)
    mine, theirs = block(0), block(2)

    def near(at, src, dst):
        return pltpu.make_async_copy(src, dst, local.at[at])

    def weight_load(s):
        return near(s, wi_in.at[s], wi_s.at[s]), near(4 + s, wo_in.at[s], wo_s.at[s])

    first = [
        near(8, ctx_in, ctx_s), near(9, wp_in, wp_s), near(10, hidden_in.at[mine], low_s)
    ]
    up_load = near(11, up_in.at[mine], up_s)
    for copy in first:
        copy.start()
    for s in range(4):
        for copy in weight_load(s):
            copy.start()
    up_load.start()

    barrier = pltpu.get_barrier_semaphore()
    for device in (core, far, diag):
        pl.semaphore_signal(barrier, inc=1, device_id=device, device_id_type=MESH)

    def greet_peer(d, carry):
        peer = (lax.rem(dp + d, count), me)
        pl.semaphore_signal(barrier, inc=1, device_id=peer, device_id_type=MESH)
        return carry

    lax.fori_loop(1, count, greet_peer, 0)

    for copy in first:
        copy.wait()
    attention = as_row(bp_ref)
    for b in range(4):
        attention = attention + dot(ctx_s[b], wp_s[b])
    middle, normed, inverse = norm_forward(
        low_s[...].astype(F32) + attention, as_row(ga_ref), as_row(sa_ref)
    )
    middle_s[...] = middle
    n1_s[...] = normed
    i1_s[...] = inverse
    mid_s[...] = middle.astype(BF16)
    sum_s[...] = jnp.zeros_like(sum_s)

    def forward_slot(s, carry):
        for copy in weight_load(s):
            copy.wait()
        pre = dot(mid_s[...], wi_s[s]) + bi_ref[s]
        phi = 0.5 * (1.0 + lax.erf(pre * math.sqrt(0.5)))
        act = (pre * phi).astype(BF16)
        act_s[s] = act
        density = jnp.exp(-0.5 * pre * pre) * (1.0 / math.sqrt(2.0 * math.pi))
        slope_s[s] = (phi + pre * density).astype(BF16)
        sum_s[...] += dot(act, wo_s[s])
        return carry

    lax.fori_loop(0, 4, forward_slot, 0)
    final, normed, inverse = norm_forward(
        middle_s[...] + sum_s[...] + as_row(bo_ref), as_row(gf_ref), as_row(sf_ref)
    )
    n2_s[...] = normed
    i2_s[...] = inverse
    out_s[...] = final.astype(BF16)
    rows = lax.broadcasted_iota(jnp.int32, (2 * PAIRS, own), 1)
    chosen = spots_ref[...] == rows
    picked_s[...] = dot(chosen.astype(F32).astype(BF16), out_s[...]).astype(BF16)

    pl.semaphore_wait(barrier, 3 + count - 1)
    out_keep = near(12, out_s, out_ref.at[mine])
    out_far = remote(out_s, out_ref.at[mine], send, recv, 7, far)
    out_core = remote(out_s, out_ref.at[mine], send, recv, 8, core)
    out_pass = remote(out_ref.at[theirs], out_ref.at[theirs], send, recv, 9, core)

    def send_out():
        out_keep.start()
        out_far.start()
        out_core.start()

    grad_cls = loss_part(
        picked_s, target_ref, loss_ref, got, every, log_s, send_l, recv_l, send_all, recv_all,
        send_out,
    )

    up_load.wait()
    grad_final = up_s[...].astype(F32) + dot(chosen.astype(F32), grad_cls, 0, 0, HIGHEST)
    normed = n2_s[...]
    grad_two = norm_backward(grad_final, normed, i2_s[...], as_row(gf_ref))
    low_s[...] = grad_two.astype(BF16)
    sum_s[...] = grad_two
    common_ref[...] = jnp.zeros_like(common_ref)
    common_ref[3:4, :] = sum_rows(low_s[...].astype(F32))
    common_ref[4:5, :] = sum_rows(grad_final * normed)
    common_ref[5:6, :] = sum_rows(grad_final)

    early = early_rows(units)
    base = 2 * units - early
    late, head, whole = slice(units, base), slice(0, units), slice(0, base)
    to_far_b = remote(mine_b.at[1], far_b, send, recv, 2, far)
    if mine_b.shape[1] > early:
        for k in range(2):
            mine_b[k, early:, :] = jnp.zeros((mine_b.shape[1] - early, D), BF16)

    def core_b(k):
        return remote(sent_b.at[k], got_b.at[k], send, recv, k, core)

    def core_a(k):
        return remote(sent_a.at[k, whole], got_a.at[k, whole], send, recv, 3 + k, core)

    def second_pair(i, carry):
        k = 1 - i
        term = dot(act_s[2 * k + 1], low_s[...], 0, 0)
        sent_b[k] = term[:early].astype(BF16)
        sent_a[k, late, :] = term[early:].astype(BF16)
        core_b(k).start()
        term = dot(act_s[2 * k], low_s[...], 0, 0)
        mine_a[k, late, :] = term[early:].astype(BF16)
        core_b(k).wait()
        mine_b[k, :early, :] = (term[:early] + got_b[k].astype(F32)).astype(BF16)

        @pl.when(i == 0)
        def _():
            to_far_b.start()

        return carry

    lax.fori_loop(0, 2, second_pair, 0)
    store_b = near(13, mine_b.at[0], sum_b)
    store_b.start()

    def first_slot(s):
        pre = (dot(low_s[...], wo_s[s], 1, 1) * slope_s[s].astype(F32)).astype(BF16)
        wide_s[s] = sum_rows(pre.astype(F32))
        sum_s[...] += dot(pre, wi_s[s], 1, 1)
        return dot(mid_s[...], pre, 0, 0)

    def first_sent(k, carry):
        sent_a[k, head, :] = first_slot(2 * k + 1).astype(BF16)
        core_a(k).start()
        return carry

    def first_kept(k, carry):
        term = first_slot(2 * k)
        core_a(k).wait()
        mine_a[k, head, :] = (term + got_a[k, head, :].astype(F32)).astype(BF16)
        mine_a[k, late, :] = add_low(mine_a[k, late, :], got_a[k, late, :])
        return carry

    lax.fori_loop(0, 2, first_sent, 0)
    lax.fori_loop(0, 2, first_kept, 0)

    out_far.wait_recv()
    out_pass.start()
    grad_middle = sum_s[...]
    normed = n1_s[...]
    grad_one = norm_backward(grad_middle, normed, i1_s[...], as_row(ga_ref))
    middle_s[...] = grad_one
    store_one = near(14, middle_s, one_out)
    store_one.start()
    low_s[...] = grad_one.astype(BF16)
    common_ref[0:1, :] = sum_rows(low_s[...].astype(F32))
    common_ref[1:2, :] = sum_rows(grad_middle * normed)
    common_ref[2:3, :] = sum_rows(grad_middle)
    rest = slice(base, sent_a.shape[1])
    to_core_p = [
        remote(sent_a.at[k, rest], got_a.at[k, rest], send, recv, 5 + k, core) for k in range(2)
    ]
    for s in (1, 3, 0, 2):
        k = s // 2
        target = sent_a if s % 2 else mine_a
        target[k, base : base + width, :] = dot(ctx_s[s], low_s[...], 0, 0).astype(BF16)
        target[k, base + width :, :] = jnp.zeros((target.shape[1] - base - width, D), BF16)
        target[k, base + width : base + width + 1, :] = wide_s[s].astype(BF16)
        if s % 2:
            to_core_p[k].start()
    for s in range(4):
        dctx_ref[s] = dot(low_s[...], wp_s[s], 1, 1).astype(BF16)
    for k in range(2):
        to_core_p[k].wait()
        mine_a[k, rest, :] = add_low(mine_a[k, rest, :], got_a[k, rest, :])
    store_a = near(15, mine_a, sum_a)
    store_a.start()
    to_far_b.wait()
    for copy in (store_b, store_a, store_one, out_keep, out_core, out_pass):
        copy.wait()
    out_far.wait_send()


def middle(ctx, wp, hidden, upstream, wi, wo, bi, vectors, spots, targets, rows_a, rows_b, dp_count):
    own, width = ctx.shape[1:]
    units = wi.shape[2]
    early = early_rows(units)
    real = -(-(2 * units - early + width + 1) // 16) * 16
    size = 2 * PAIRS
    shape = jax.ShapeDtypeStruct
    vmem = pltpu.VMEM
    dma = pltpu.SemaphoreType.DMA
    return pl.pallas_call(
        middle_kernel,
        out_shape=[
            shape(hidden.shape, BF16),
            shape((own, D), F32),
            shape((4, own, width), BF16),
            shape((2, rows_a, D), BF16),
            shape((rows_b, D), BF16),
            shape((rows_b, D), BF16),
            shape((8, D), F32),
            shape((1, 1), F32),
        ],
        in_specs=[ANY] * 6 + [VMEM] * 9,
        out_specs=[ANY, ANY, VMEM, ANY, ANY, ANY, VMEM, VMEM],
        scratch_shapes=[
            vmem((4, own, width), BF16),
            vmem((4, width, D), BF16),
            vmem((own, D), BF16),
            vmem((own, D), BF16),
            vmem((4, D, units), BF16),
            vmem((4, units, D), BF16),
            vmem((4, own, units), BF16),
            vmem((4, own, units), BF16),
            vmem((own, D), BF16),
            vmem((own, D), F32),
            vmem((own, 1), F32),
            vmem((own, D), F32),
            vmem((own, 1), F32),
            vmem((own, D), F32),
            vmem((own, D), F32),
            vmem((own, D), BF16),
            vmem((4, 1, units), F32),
            vmem((2, rows_a, D), BF16),
            vmem((2, real, D), BF16),
            vmem((2, real, D), BF16),
            vmem((2, rows_b, D), BF16),
            vmem((2, early, D), BF16),
            vmem((2, early, D), BF16),
            vmem((size, D), BF16),
            vmem((4, size, D), BF16),
            vmem((2, dp_count, size, D), BF16),
            vmem((1, dp_count * 2 * size), F32),
            dma((10,)),
            dma((10,)),
            dma((16,)),
            dma((4,)),
            dma((4,)),
            dma((dp_count,)),
            dma((dp_count,)),
        ],
        compiler_params=pltpu.CompilerParams(
            collective_id=1, has_side_effects=True, vmem_limit_bytes=63 << 20
        ),
        cost_estimate=pl.CostEstimate(
            flops=18 * 10**9, bytes_accessed=40 << 20, transcendentals=1 << 22
        ),
        name="middle",
    )(ctx, wp, hidden, upstream, wi, wo, bi, *vectors, spots, targets)


BACKWARD_TASKS = (0, 1, 3, 4, 6, 7, 8, 8, 9, 11, 12, 14, 15, 15)


def ring_place(index, count):
    upper = index // 2
    return upper + (index % 2) * (count - 1 - 2 * upper)


def ring_index(place, count):
    return jnp.where(place < count // 2, 2 * place, 2 * (count - 1 - place) + 1)


def backward_kernel(
    hidden_in, q_in, k_in, v_in, wq_ref, wk_ref, wv_ref, seg_ref, dctx_in, one_in, common_ref,
    sum_a, sum_b, far_b,
    grad_ref, sums_ref,
    hidden_ref, q_ref, k_ref, v_ref, one_ref, low_s,
    dctx_s, dk_s, dv_s, dq_s, dw_s, dx_s, dx_core, dx_far, common_s,
    work_a, work_b, far_half, ring_a, ring_f, ring_b, tail, ring_q, far_s,
    send, recv, local, *sems,
):
    dp, me = lax.axis_index("dp"), lax.axis_index("mp")
    count = lax.axis_size("dp")
    tokens, width = q_ref.shape
    own = tokens // 4
    heads = width // HEAD_DIM
    chunk_a, chunk_b = work_a.shape[1] // count, work_b.shape[0] // count
    rows_f = chunk_a + chunk_b
    rows_q = sums_ref.shape[1] - rows_f
    half = D // 2
    core, far, diag = (dp, me ^ 1), (dp, me ^ 2), (dp, me ^ 3)
    place = ring_place(dp, count)
    ahead = (ring_index(lax.rem(place + 1, count), count), me)
    behind = (ring_index(lax.rem(place + count - 1, count), count), me)
    used_sems = [0]

    def to(src, dst, device):
        used_sems[0] += 1
        return remote(src, dst, send, recv, used_sems[0] - 1, device)

    used_local = [0]

    def near(src, dst):
        used_local[0] += 1
        return pltpu.make_async_copy(src, dst, local.at[used_local[0] - 1])

    def block(b):
        return pl.ds(pl.multiple_of((me ^ b) * own, own), own)

    mine, theirs = block(0), block(2)
    greet([core, far, diag, ahead, behind])
    dctx_copies = [to(dctx_in.at[b], dctx_s.at[mine], (dp, me ^ b)) for b in (2, 3, 1)]
    dctx_keep = near(dctx_in.at[0], dctx_s.at[mine])
    loads = [near(sum_a, work_a), near(sum_b, work_b), near(far_b, far_half)]
    common_copies = [to(common_ref, common_s.at[b], (dp, me ^ b)) for b in (1, 2, 3)]
    fetches = [
        near(src, dst)
        for src, dst in (
            (q_in, q_ref), (k_in, k_ref), (v_in, v_ref), (hidden_in, hidden_ref), (one_in, one_ref)
        )
    ]
    for copy in dctx_copies + [dctx_keep] + loads + common_copies + fetches:
        copy.start()
    dw_s[...] = jnp.zeros_like(dw_s)
    common_s[0] = common_ref[...]

    def lanes(d):
        return slice(d * half, (d + 1) * half)

    def sent(d, s):
        return lax.rem(place + (count - 1 - s if d == 0 else 1 + s), count)

    def rows_at(c, rows):
        return pl.ds(pl.multiple_of(c * rows, 16), rows)

    def ring_copy(src, dst, sems, s, d):
        return pltpu.make_async_remote_copy(
            src_ref=src,
            dst_ref=dst,
            send_sem=sems[0].at[s, d],
            recv_sem=sems[1].at[s, d],
            device_id=ahead if d == 0 else behind,
            device_id_type=MESH,
        )

    def make_ring(buffer, sems, terms):
        def copy(s, d):
            return ring_copy(buffer.at[s, d], buffer.at[s + 1, d], sems, s, d)

        def step(s):
            for d in range(2):
                now = terms(sent(d, s), d)
                if isinstance(s, int) and s == 0:
                    buffer[0, d] = now
                else:
                    copy(s - 1, d).wait_recv()
                    buffer[s, d] = add_low(buffer[s, d], now)
                copy(s, d).start()

        def last(d):
            copy(count - 2, d).wait_recv()
            return buffer[count - 1, d].astype(F32) + terms(place, d).astype(F32)

        return copy, step, last

    copy_a, step_a, last_a = make_ring(
        ring_a, sems[0:2], lambda c, d: work_a[0, rows_at(c, chunk_a), lanes(d)]
    )
    copy_f, step_f, last_f = make_ring(
        ring_f, sems[2:4], lambda c, d: work_a[1, rows_at(c, chunk_a), lanes(d)]
    )
    copy_b, step_b, last_b = make_ring(
        ring_b, sems[4:6], lambda c, d: work_b[rows_at(c, chunk_b), lanes(d)]
    )
    copy_q, step_q, last_q = make_ring(
        ring_q, sems[6:8], lambda c, d: tail[rows_at(c, rows_q), lanes(d)]
    )
    far_copy = to(far_s.at[0], far_s.at[1], far)

    def begin():
        for copy in loads:
            copy.wait()
        step_f(0)
        step_a(0)

        def body(c, carry):
            at = rows_at(c, chunk_b)
            work_b[at, :] = add_low(work_b[at, :], far_half[at, :])
            return carry

        lax.fori_loop(0, count, body, 0)
        step_b(0)

    def steps_ab(s):
        step_a(s)
        step_b(s)

    def end_f():
        for d in range(2):
            far_s[0, :, lanes(d)] = last_f(d).astype(BF16)
        far_copy.start()

    def end_ab():
        for d in range(2):
            work_a[0, rows_at(place, chunk_a), lanes(d)] = last_a(d).astype(BF16)
            sums_ref[place, chunk_a:rows_f, lanes(d)] = last_b(d).astype(BF16)
        start_b(0)

    def groups(step, most):
        calls = []
        parts = min(count - 2, most)
        for g in range(parts):
            low, high = 1 + g * (count - 2) // parts, 1 + (g + 1) * (count - 2) // parts
            if high - low == 1:
                calls.append(partial(step, low))
            else:

                def many(low=low, high=high):
                    def body(s, carry):
                        step(s)
                        return carry

                    lax.fori_loop(low, high, body, 0)

                calls.append(many)
        return calls

    def mixed(*lists):
        return [task for tasks in zip(*lists) for task in tasks]

    todo = mixed(groups(step_f, 6), groups(steps_ab, 6)) + [end_f, end_ab]

    def advance():
        if todo:
            todo.pop(0)()

    def make_gather(rows, sems):
        def view(c, d):
            return sums_ref.at[c, rows, lanes(d)]

        def copy(s, d):
            ref = view(lax.rem(place + (count - s if d == 0 else s), count), d)
            return ring_copy(ref, ref, sems, s, d)

        def arrival(s, d):
            ref = view(sent(d, s), d)
            return ring_copy(ref, ref, sems, s, d)

        def start(s):
            for d in range(2):
                copy(s, d).start()

        def finish(s):
            for d in range(2):
                arrival(s, d).wait_recv()

        def step(s):
            finish(s - 1)
            start(s)

        return copy, start, step, finish

    copy_g, start_g, step_g, finish_g = make_gather(slice(0, chunk_a), sems[8:10])
    copy_e, start_b, step_e, finish_e = make_gather(slice(chunk_a, rows_f), sems[10:12])
    copy_h, start_h, step_h, finish_h = make_gather(slice(rows_f, rows_f + rows_q), sems[12:14])

    def begin_g():
        far_copy.wait()
        sums_ref[place, 0:chunk_a, :] = add_low(work_a[0, rows_at(place, chunk_a), :], far_s[1])
        start_g(0)

    gathers = mixed([begin_g] + groups(step_g, 6), groups(step_e, 6) + [lambda: finish_e(count - 2)])

    masks, masks_f = head_masks(heads, BF16), head_masks(heads, F32)

    def attend(row, b):
        keys = pl.ds(pl.multiple_of(row * LEN, LEN), LEN)
        at = pl.ds(pl.multiple_of(row * LEN + b * BLOCK, BLOCK), BLOCK)
        q3 = stack_heads(q_ref[at, :], masks)
        d3 = stack_heads(dctx_s[at, :], masks)
        scores = dot(q3, k_ref[keys, :], 1, 1)
        same = same_segment(seg_ref.at[row], pl.multiple_of(b * BLOCK, BLOCK), slice(None))
        probs = masked_soft(scores, same, heads)
        grad_probs = dot(d3, v_ref[keys, :], 1, 1)
        centre = jnp.sum(probs * grad_probs, axis=-1, keepdims=True)
        grad_scores = (probs * (grad_probs - centre)).astype(BF16)
        dq = merge_heads(dot(grad_scores, k_ref[keys, :]), masks_f).astype(BF16)
        here = pl.ds(pl.multiple_of(b * BLOCK, BLOCK), BLOCK)
        dq_s[here, :] = dq * BF16(1.0 / math.sqrt(HEAD_DIM))
        dk_s[...] += dot(grad_scores, q3, 0, 0)
        dv_s[...] += dot(probs.astype(BF16), d3, 0, 0)

    def weight_terms(dq, dk, dv, rows):
        dw_s[0:width, :] += dot(dq, rows, 0, 0)
        dw_s[width : 2 * width, :] += dot(dk, rows, 0, 0)
        dw_s[2 * width : 3 * width, :] += dot(dv, rows, 0, 0)
        dw_s[3 * width : 3 * width + 1, 0:width] += sum_rows(dq.astype(F32))
        dw_s[3 * width + 1 : 3 * width + 2, 0:width] += sum_rows(dv.astype(F32))

    begin()
    for copy in dctx_copies + [dctx_keep] + fetches:
        copy.wait()
    first_row = 1 - me // 2
    side = me % 2
    blocks = LEN // BLOCK
    dx_core_far = to(dx_s.at[3], dx_core.at[0], core)
    dx_to_far = to(dx_s.at[2], dx_far, far)
    dx_core_near = to(dx_s.at[1], dx_core.at[1], core)

    def pass_far():
        dx_core_far.wait()
        dx_s[2] = add_low(dx_s[2], dx_core[0])
        dx_to_far.start()

    def begin_q():
        used = 3 * width + 2
        tail[0:used, :] = dw_s[0:used, :].astype(BF16)
        tail[used:, :] = jnp.zeros((tail.shape[0] - used, D), BF16)
        for copy in common_copies:
            copy.wait()
        common = (common_s[0] + common_s[1]) + (common_s[2] + common_s[3])
        tail[3 * width + 16 : 3 * width + 24, :] = common.astype(BF16)
        step_q(0)

    schedule = {blocks: [pass_far]}
    for at in BACKWARD_TASKS:
        if todo:
            schedule.setdefault(at, []).append(todo.pop(0))

    def row_step(i, carry):
        row = first_row + i * (1 - 2 * first_row)
        dk_s[...] = jnp.zeros_like(dk_s)
        dv_s[...] = jnp.zeros_like(dv_s)

        def block_step(b, inner):
            attend(row, b)
            for when, tasks in schedule.items():

                @pl.when(i * blocks + b == when)
                def _(tasks=tasks):
                    for act in tasks:
                        act()

            return inner

        lax.fori_loop(0, blocks, block_step, 0)
        rows = hidden_ref[pl.ds(pl.multiple_of(row * LEN, LEN), LEN), :]
        dq, dk, dv = dq_s[...], dk_s[...].astype(BF16), dv_s[...].astype(BF16)
        weight_terms(dq, dk, dv, rows)

        @pl.when(i == 1)
        def _():
            begin_q()

        dx = (dot(dq, wq_ref[...]) + dot(dk, wk_ref[...]) + dot(dv, wv_ref[...])).astype(BF16)
        slot = 2 - 2 * i
        dx_s[slot + side] = dx[:own]
        dx_s[slot + 1 - side] = dx[own:]

        @pl.when(i == 0)
        def _():
            dx_core_far.start()

        @pl.when(i == 1)
        def _():
            dx_core_near.start()

        return carry

    lax.fori_loop(0, 2, row_step, 0)
    later = groups(step_q, 6)
    for tasks in (todo, later, gathers):
        while tasks and (tasks is todo or len(tasks) > 5 + 8 * (tasks is gathers)):
            tasks.pop(0)()
    dx_core_near.wait()
    dx_to_far.wait()
    low_s[...] = (
        one_ref[...]
        + dx_s[0].astype(F32)
        + dx_core[1].astype(F32)
        + dx_far[...].astype(F32)
    ).astype(BF16)
    grad_keep = near(low_s, grad_ref.at[mine])
    grad_far = to(low_s, grad_ref.at[mine], far)
    grad_core = to(low_s, grad_ref.at[mine], core)
    grad_pass = to(grad_ref.at[theirs], grad_ref.at[theirs], core)
    grad_keep.start()
    grad_far.start()
    grad_core.start()
    def begin_h():
        for d in range(2):
            sums_ref[place, rows_f:, lanes(d)] = last_q(d).astype(BF16)
        start_h(0)

    later += [begin_h] + groups(step_h, 6)
    while later or gathers:
        for tasks in (later, gathers):
            if tasks:
                tasks.pop(0)()
    finish_g(count - 2)
    finish_h(count - 2)
    grad_far.wait_recv()
    grad_pass.start()
    for copy in (grad_core, grad_pass, grad_keep):
        copy.wait()
    grad_far.wait_send()

    def drain(s, carry):
        for d in range(2):
            for copy in (copy_a, copy_f, copy_b, copy_q, copy_g, copy_e, copy_h):
                copy(s, d).wait_send()
        return carry

    lax.fori_loop(0, count - 1, drain, 0)


def backward_attention(
    hidden, q, k, v, wq, wk, wv, seg, dctx, one, common, sum_a, sum_b, far_b,
    dp_count, rows_q
):
    tokens, width = q.shape
    own = tokens // 4
    rows_a, rows_b = sum_a.shape[1], sum_b.shape[0]
    chunk_a, chunk_b = rows_a // dp_count, rows_b // dp_count
    shape = jax.ShapeDtypeStruct
    steps = (dp_count - 1, 2)
    dma = pltpu.SemaphoreType.DMA
    return pl.pallas_call(
        backward_kernel,
        out_shape=[
            shape((tokens, D), BF16),
            shape((dp_count, chunk_a + chunk_b + rows_q, D), BF16),
        ],
        in_specs=[ANY] * 4 + [VMEM] * 4 + [ANY, ANY, VMEM] + [ANY] * 3,
        out_specs=[ANY, VMEM],
        scratch_shapes=[
            pltpu.VMEM((tokens, D), BF16),
            pltpu.VMEM((tokens, width), BF16),
            pltpu.VMEM((tokens, width), BF16),
            pltpu.VMEM((tokens, width), BF16),
            pltpu.VMEM((own, D), F32),
            pltpu.VMEM((own, D), BF16),
            pltpu.VMEM((tokens, width), BF16),
            pltpu.VMEM((LEN, width), F32),
            pltpu.VMEM((LEN, width), F32),
            pltpu.VMEM((LEN, width), BF16),
            pltpu.VMEM((3 * width + 16, D), F32),
            pltpu.VMEM((4, own, D), BF16),
            pltpu.VMEM((2, own, D), BF16),
            pltpu.VMEM((own, D), BF16),
            pltpu.VMEM((4, 8, D), F32),
            pltpu.VMEM((2, rows_a, D), BF16),
            pltpu.VMEM((rows_b, D), BF16),
            pltpu.VMEM((rows_b, D), BF16),
            pltpu.VMEM((dp_count, 2, chunk_a, D // 2), BF16),
            pltpu.VMEM((dp_count, 2, chunk_a, D // 2), BF16),
            pltpu.VMEM((dp_count, 2, chunk_b, D // 2), BF16),
            pltpu.VMEM((dp_count * rows_q, D), BF16),
            pltpu.VMEM((dp_count, 2, rows_q, D // 2), BF16),
            pltpu.VMEM((2, chunk_a, D), BF16),
            dma((21,)),
            dma((21,)),
            dma((12,)),
        ]
        + [dma(steps)] * 14,
        compiler_params=pltpu.CompilerParams(
            collective_id=2, has_side_effects=True, vmem_limit_bytes=62 << 20
        ),
        cost_estimate=pl.CostEstimate(
            flops=24 * 10**9, bytes_accessed=40 << 20, transcendentals=1 << 23
        ),
        name="backward_attention",
    )(hidden, q, k, v, wq, wk, wv, seg, dctx, one, common, sum_a, sum_b, far_b)


def padded(rows, dp_count):
    return -(-rows // (16 * dp_count)) * 16


def on_device(
    hidden,
    upstream,
    segment_ids,
    cls_positions,
    positives,
    w_query,
    b_query,
    w_key,
    w_value,
    b_value,
    w_out,
    b_out,
    gain_attn,
    shift_attn,
    w_inner,
    b_inner,
    w_outer,
    b_outer,
    gain_final,
    shift_final,
):
    tokens = hidden.shape[0]
    row_count = tokens // LEN
    width = w_query.shape[1]
    units = w_inner.shape[1]
    dp_count = lax.axis_size("dp")
    me, shares = lax.axis_index("mp"), lax.axis_size("mp")
    own = tokens // shares
    segment_rows = segment_ids.reshape(row_count, LEN)
    seg_row = segment_rows[:, None, :]

    query_rows, key_rows, value_rows, ctx, wi_all, wo_all, wp_all, bi_all = forward_attention(
        hidden,
        w_query.T,
        b_query.reshape(1, -1),
        w_key.T,
        w_value.T,
        b_value.reshape(1, -1),
        seg_row,
        w_inner,
        w_outer,
        w_out,
        b_inner,
    )

    own_row = me * own // LEN
    spots = lax.dynamic_slice_in_dim(cls_positions, own_row, 1, 0)[0] - (me * own - own_row * LEN)
    spots = spots[:, None]
    vectors = (b_out, b_outer, gain_attn, shift_attn, gain_final, shift_final)
    group = positives // PAIRS
    column = (group % row_count * dp_count + group // row_count) * (2 * PAIRS) + PAIRS
    column = (column + positives % PAIRS).reshape(dp_count, row_count, PAIRS).swapaxes(0, 1)
    targets = jnp.concatenate([column, jnp.full_like(column, -1)], axis=2).reshape(1, -1)
    early = early_rows(units)
    base = 2 * units - early
    rows_a = padded(base + width + 1, dp_count) * dp_count
    rows_b = padded(early, dp_count) * dp_count
    layer_out, grad_one, dctx, sum_a, sum_b, far_b, common, mean_loss = middle(
        ctx, wp_all, hidden, upstream, wi_all, wo_all, bi_all, vectors, spots, targets,
        rows_a, rows_b, dp_count,
    )

    rows_q = padded(3 * width + 24, dp_count)
    grad_low, sums = backward_attention(
        hidden, query_rows, key_rows, value_rows, w_query.T, w_key.T, w_value.T, seg_row, dctx, grad_one,
        common, sum_a, sum_b, far_b, dp_count, rows_q,
    )
    chunk_a, rows_f = rows_a // dp_count, (rows_a + rows_b) // dp_count
    sums_a = sums[:, :chunk_a].reshape(-1, D)
    sums_b = sums[:, chunk_a:rows_f].reshape(-1, D)
    sums_q = sums[:, rows_f:].reshape(-1, D)
    sums_p = sums_a[base : base + width + 1].astype(F32)
    sums_o = jnp.concatenate([sums_b[:early], sums_a[units:base]], axis=0)
    small = sums_q[3 * width :].astype(F32)
    return (
        mean_loss.reshape(1),
        layer_out,
        grad_low.astype(F32),
        sums_q[:width].astype(F32).T,
        small[0, :width],
        sums_q[width : 2 * width].astype(F32).T,
        sums_q[2 * width : 3 * width].astype(F32).T,
        small[1, :width],
        sums_p[:width],
        small[16],
        small[17],
        small[18],
        sums_a[:units].astype(F32),
        sums_p[width],
        sums_o.astype(F32),
        small[19],
        small[20],
        small[21],
    )


def solution(mesh):
    return jax.shard_map(
        on_device,
        mesh=mesh,
        in_specs=(
            P("dp", None),
            P("dp", None),
            P("dp"),
            P("dp", None),
            P(),
            P(None, "mp"),
            P("mp"),
            P(None, "mp"),
            P(None, "mp"),
            P("mp"),
            P("mp", None),
            P(),
            P(),
            P(),
            P(None, "mp"),
            P("mp"),
            P("mp", None),
            P(),
            P(),
            P(),
        ),
        out_specs=(
            P(),
            P("dp", None),
            P("dp", None),
            P(None, "mp"),
            P("mp"),
            P(None, "mp"),
            P(None, "mp"),
            P("mp"),
            P("mp", None),
            P(),
            P(),
            P(),
            P(None, "mp"),
            P("mp"),
            P("mp", None),
            P(),
            P(),
            P(),
        ),
        check_vma=False,
    )
```

profile of v0, /device:TPU:0, one launch (start us, length us, event | category | flops | bytes accessed | tf_op | source)
XLA Modules:
  0.0 236.3 jit_solution(1247756896729784468)
XLA Ops:
  0.7 0.7 subtract_bitcast_fusion
  1.4 0.7 fusion
  2.0 0.1 reshape.74
  2.2 0.6 reshape.75.target_ref
  2.8 0.7 copy.39.spots_ref
  3.5 42.3 %forward_attention.1 = (bf16[2048,192]{1,0:T(8,128)(2,1)}, bf16[2048,192]{1,0:T(8,128)(2,1)}, bf16[2048,192]{1,0:T(8,128)(2,1)}, bf16[4,512,192]{2,1,0:T(8,128)(...) custom-call(bf16[2048,768]{1,0:T(8,128)(2,1)} %hidden_in.3, ...), custom_call_target="tpu_custom_call" | custom-call | flops 8000000000 | bytes 25165824 | tf_op jit(solution)/shard_map/forward_attention/pallas_call | solution.py:287
  45.8 52.6 %middle.1 = (bf16[2048,768]{1,0:T(8,128)(2,1)}, f32[512,768]{1,0:T(8,128)}, bf16[4,512,192]{2,1,0:T(8,128)(2,1)}, bf16[2,1280,768]{2,1,0:T(8,128)(2,1)}, bf16[51...) custom-call(bf16[4,512,192]{2,1,0:T(8,128)(2,1)} %get-tuple-element.36.ctx_in, ...), custom_call_target="tpu_custom_call" | custom-call | flops 17999998976 | bytes 41943040 | tf_op jit(solution)/shard_map/middle/pallas_call | solution.py:615
  98.3 120.5 %backward_attention.1 = (bf16[2048,768]{1,0:T(8,128)(2,1)}, bf16[8,304,768]{2,1,0:T(8,128)(2,1)}) custom-call(bf16[2048,768]{1,0:T(8,128)(2,1)} %hidden_in.3, bf16[2048,192]{1,0:T(8,128)(2,1)} %get-tuple-element.43.q_in, bf16[2048,192]{1,0:T(8,128)(2,1)} %get-tuple-element.44.k_in, bf16[2048,192]{1,0:T(8,128)(2,1)} %get-tuple-element.45.v_in, ...), custom_call_target="tpu_custom_call" | custom-call | flops 24000000000 | bytes 41943040 | tf_op jit(solution)/shard_map/backward_attention/pallas_call | solution.py:1042
  218.8 1.2 slice.75
  220.0 1.3 slice.60
  221.3 1.7 slice.67
  223.0 0.6 fusion.3
  223.7 0.7 slice_reduce_fusion
  224.3 0.9 slice.87
  225.2 1.2 convert_bitcast_fusion
  226.4 0.0 copy-start.1
  226.4 2.6 %slice_convert_fusion = (f32[768,768]{1,0:T(8,128)}, f32[768,768]{1,0:T(8,128)}) fusion(bf16[1280,768]{1,0:T(8,128)(2,1)S(1)} %bitcast.23, bf16[256,768]{1,0:T(8,128)(2,1)S(1)} %slice.93, bf16[512,768]{1,0:T(8,128)(2,1)S(1)} %bitcast.26), kind=kLoop, calls=%fused_computation | loop fusion | flops 2949120 | bytes 7077888 | tf_op jit(solution)/shard_map/convert_element_type | solution.py:1182
  229.0 0.7 copy-done.1
  229.7 0.0 copy-start
  229.7 3.2 %convert_element_type.18 = f32[2048,768]{1,0:T(8,128)} convert(bf16[2048,768]{1,0:T(8,128)(2,1)S(1)} %copy-done.1) | non-fusion elementwise | flops 1572864 | bytes 9437184 | tf_op jit(solution)/shard_map/convert_element_type | solution.py:1172
  233.5 0.0 copy-done
  233.5 1.7 copy.44
  (5 shorter events, 0.1 us)
Async XLA Ops:
  226.4 3.3 %copy-start.1 = (bf16[2048,768]{1,0:T(8,128)(2,1)S(1)}, bf16[2048,768]{1,0:T(8,128)(2,1)}, u32[]{:S(2)}) copy-start(bf16[2048,768]{1,0:T(8,128)(2,1)} %get-tuple-element.52) | copy-start | bytes 9437188
  229.7 3.8 %copy-start = (bf16[2048,768]{1,0:T(8,128)(2,1)S(1)}, bf16[2048,768]{1,0:T(8,128)(2,1)}, u32[]{:S(2)}) copy-start(bf16[2048,768]{1,0:T(8,128)(2,1)} %get-tuple-element.87) | copy-start | bytes 9437188
where the time goes:
time: 237 us; the launch traced here: 236 us
  Pallas kernels  215 us (91%)
  local copies, waits for them, and re-layouts  10 us (4%)
  other arithmetic  8.48 us (4%)
  between operations  2.46 us (1%)
    pallas_call x1, Pallas kernels, backward_attention(): pl.pallas_call(backward_kernel, out_shape=[shape((tokens, D), BF16), shap...  121 us
    pallas_call x1, Pallas kernels, middle(): pl.pallas_call(middle_kernel, out_shape=[shape(hidden.shape, BF16), shape...  52.6 us
    pallas_call x1, Pallas kernels, forward_attention(): pl.pallas_call(forward_kernel, out_shape=[shape((tokens, width), BF16)] *...  42.3 us

commit v1 on v0

--- a/solution.py
+++ b/solution.py
@@ -77,11 +77,22 @@
 
 
 def masked_soft(scores, same, heads):
+    parts, logs = [], []
+    for h in range(heads):
+        part = jnp.where(same, scores[h * BLOCK : (h + 1) * BLOCK], -1e30)
+        largest = jnp.max(part, axis=-1, keepdims=True)
+        part = jnp.exp(part - largest)
+        total = jnp.sum(part, axis=-1, keepdims=True)
+        parts.append(part * (1.0 / total))
+        logs.append(largest + jnp.log(total))
+    return jnp.concatenate(parts, axis=0), jnp.concatenate(logs, axis=0)
+
+
+def soft_again(scores, same, logs, heads):
     parts = []
     for h in range(heads):
-        part = jnp.where(same, scores[h * BLOCK : (h + 1) * BLOCK], -1e30)
-        part = jnp.exp(part - jnp.max(part, axis=-1, keepdims=True))
-        parts.append(part * (1.0 / jnp.sum(part, axis=-1, keepdims=True)))
+        rows = slice(h * BLOCK, (h + 1) * BLOCK)
+        parts.append(jnp.exp(jnp.where(same, scores[rows], -1e30) - logs[rows]))
     return jnp.concatenate(parts, axis=0)
 
 
@@ -110,7 +121,7 @@
 
 def forward_kernel(
     hidden_ref, wq_ref, bq_ref, wk_ref, wv_ref, bv_ref, seg_ref, wi_ref, wo_ref, wp_ref, bi_ref,
-    q_ref, k_ref, v_ref, ctx_ref, wi_all, wo_all, wp_all, bi_all,
+    q_ref, k_ref, v_ref, log_ref, ctx_ref, wi_all, wo_all, wp_all, bi_all,
     ctx_s, send, recv, local,
 ):
     dp, me = lax.axis_index("dp"), lax.axis_index("mp")
@@ -206,8 +217,10 @@
         q3 = stack_heads(q_ref[at, :], masks)
         scores = dot(q3, k_ref[keys, :], 1, 1)
         same = same_segment(seg_ref.at[row], pl.multiple_of(b * BLOCK, BLOCK), slice(None))
-        weights = masked_soft(scores, same, heads).astype(BF16)
-        ctx_s[at, :] = merge_heads(dot(weights, v_ref[keys, :]), masks_f).astype(BF16)
+        weights, logs = masked_soft(scores, same, heads)
+        log_ref[row, b] = logs
+        out3 = dot(weights.astype(BF16), v_ref[keys, :])
+        ctx_s[at, :] = merge_heads(out3, masks_f).astype(BF16)
 
     def got_x(i):
         x_copies[i].wait_recv()
@@ -288,6 +301,7 @@
         forward_kernel,
         out_shape=[shape((tokens, width), BF16)] * 3
         + [
+            shape((tokens // LEN, LEN // BLOCK, width // HEAD_DIM * BLOCK, 1), F32),
             shape((4, tokens // 4, width), BF16),
             shape((4, D, units), BF16),
             shape((4, units, D), BF16),
@@ -295,7 +309,7 @@
             shape((4, 1, units), F32),
         ],
         in_specs=[VMEM] * 11,
-        out_specs=[VMEM] * 4 + [ANY, ANY, ANY, VMEM],
+        out_specs=[VMEM] * 5 + [ANY, ANY, ANY, VMEM],
         scratch_shapes=[
             pltpu.VMEM((tokens, width), BF16),
             pltpu.SemaphoreType.DMA((copies,)),
@@ -685,10 +699,10 @@
 
 
 def backward_kernel(
-    hidden_in, q_in, k_in, v_in, wq_ref, wk_ref, wv_ref, seg_ref, dctx_in, one_in, common_ref,
+    hidden_in, q_in, k_in, v_in, log_in, wq_ref, wk_ref, wv_ref, seg_ref, dctx_in, one_in, common_ref,
     sum_a, sum_b, far_b,
-    grad_ref, sums_ref,
-    hidden_ref, q_ref, k_ref, v_ref, one_ref, low_s,
+    grad_ref, done_a, done_b, done_q,
+    hidden_ref, q_ref, k_ref, v_ref, log_ref, prob_s, one_ref, low_s,
     dctx_s, dk_s, dv_s, dq_s, dw_s, dx_s, dx_core, dx_far, common_s,
     work_a, work_b, far_half, ring_a, ring_f, ring_b, tail, ring_q, far_s,
     send, recv, local, *sems,
@@ -699,8 +713,7 @@
     own = tokens // 4
     heads = width // HEAD_DIM
     chunk_a, chunk_b = work_a.shape[1] // count, work_b.shape[0] // count
-    rows_f = chunk_a + chunk_b
-    rows_q = sums_ref.shape[1] - rows_f
+    rows_q = done_q.shape[0] // count
     half = D // 2
     core, far, diag = (dp, me ^ 1), (dp, me ^ 2), (dp, me ^ 3)
     place = ring_place(dp, count)
@@ -730,7 +743,8 @@
     fetches = [
         near(src, dst)
         for src, dst in (
-            (q_in, q_ref), (k_in, k_ref), (v_in, v_ref), (hidden_in, hidden_ref), (one_in, one_ref)
+            (q_in, q_ref), (k_in, k_ref), (log_in, log_ref), (v_in, v_ref), (hidden_in, hidden_ref),
+            (one_in, one_ref),
         )
     ]
     for copy in dctx_copies + [dctx_keep] + loads + common_copies + fetches:
@@ -817,7 +831,7 @@
     def end_ab():
         for d in range(2):
             work_a[0, rows_at(place, chunk_a), lanes(d)] = last_a(d).astype(BF16)
-            sums_ref[place, chunk_a:rows_f, lanes(d)] = last_b(d).astype(BF16)
+            done_b[rows_at(place, chunk_b), lanes(d)] = last_b(d).astype(BF16)
         start_b(0)
 
     def groups(step, most):
@@ -848,9 +862,9 @@
         if todo:
             todo.pop(0)()
 
-    def make_gather(rows, sems):
+    def make_gather(done, rows, sems):
         def view(c, d):
-            return sums_ref.at[c, rows, lanes(d)]
+            return done.at[rows_at(c, rows), lanes(d)]
 
         def copy(s, d):
             ref = view(lax.rem(place + (count - s if d == 0 else s), count), d)
@@ -874,35 +888,45 @@
 
         return copy, start, step, finish
 
-    copy_g, start_g, step_g, finish_g = make_gather(slice(0, chunk_a), sems[8:10])
-    copy_e, start_b, step_e, finish_e = make_gather(slice(chunk_a, rows_f), sems[10:12])
-    copy_h, start_h, step_h, finish_h = make_gather(slice(rows_f, rows_f + rows_q), sems[12:14])
+    copy_g, start_g, step_g, finish_g = make_gather(done_a, chunk_a, sems[8:10])
+    copy_e, start_b, step_e, finish_e = make_gather(done_b, chunk_b, sems[10:12])
+    copy_h, start_h, step_h, finish_h = make_gather(done_q, rows_q, sems[12:14])
 
     def begin_g():
         far_copy.wait()
-        sums_ref[place, 0:chunk_a, :] = add_low(work_a[0, rows_at(place, chunk_a), :], far_s[1])
+        at = rows_at(place, chunk_a)
+        done_a[at, :] = add_low(work_a[0, at, :], far_s[1])
         start_g(0)
 
     gathers = mixed([begin_g] + groups(step_g, 6), groups(step_e, 6) + [lambda: finish_e(count - 2)])
 
     masks, masks_f = head_masks(heads, BF16), head_masks(heads, F32)
 
+    def at_block(row, b):
+        return (
+            pl.ds(pl.multiple_of(row * LEN + b * BLOCK, BLOCK), BLOCK),
+            pl.ds(pl.multiple_of(row * LEN, LEN), LEN),
+        )
+
+    def probabilities(row, b):
+        at, keys = at_block(row, b)
+        scores = dot(stack_heads(q_ref[at, :], masks), k_ref[keys, :], 1, 1)
+        same = same_segment(seg_ref.at[row], pl.multiple_of(b * BLOCK, BLOCK), slice(None))
+        prob_s[b] = soft_again(scores, same, log_ref[row, b], heads).astype(BF16)
+
     def attend(row, b):
-        keys = pl.ds(pl.multiple_of(row * LEN, LEN), LEN)
-        at = pl.ds(pl.multiple_of(row * LEN + b * BLOCK, BLOCK), BLOCK)
+        at, keys = at_block(row, b)
         q3 = stack_heads(q_ref[at, :], masks)
         d3 = stack_heads(dctx_s[at, :], masks)
-        scores = dot(q3, k_ref[keys, :], 1, 1)
-        same = same_segment(seg_ref.at[row], pl.multiple_of(b * BLOCK, BLOCK), slice(None))
-        probs = masked_soft(scores, same, heads)
         grad_probs = dot(d3, v_ref[keys, :], 1, 1)
+        probs = prob_s[b].astype(F32)
         centre = jnp.sum(probs * grad_probs, axis=-1, keepdims=True)
         grad_scores = (probs * (grad_probs - centre)).astype(BF16)
         dq = merge_heads(dot(grad_scores, k_ref[keys, :]), masks_f).astype(BF16)
         here = pl.ds(pl.multiple_of(b * BLOCK, BLOCK), BLOCK)
         dq_s[here, :] = dq * BF16(1.0 / math.sqrt(HEAD_DIM))
         dk_s[...] += dot(grad_scores, q3, 0, 0)
-        dv_s[...] += dot(probs.astype(BF16), d3, 0, 0)
+        dv_s[...] += dot(prob_s[b], d3, 0, 0)
 
     def weight_terms(dq, dk, dv, rows):
         dw_s[0:width, :] += dot(dq, rows, 0, 0)
@@ -912,10 +936,18 @@
         dw_s[3 * width + 1 : 3 * width + 2, 0:width] += sum_rows(dv.astype(F32))
 
     begin()
-    for copy in dctx_copies + [dctx_keep] + fetches:
-        copy.wait()
     first_row = 1 - me // 2
     side = me % 2
+    for copy in fetches[:3]:
+        copy.wait()
+
+    def early_block(b, carry):
+        probabilities(first_row, b)
+        return carry
+
+    lax.fori_loop(0, LEN // BLOCK, early_block, 0)
+    for copy in dctx_copies + [dctx_keep] + fetches[3:]:
+        copy.wait()
     blocks = LEN // BLOCK
     dx_core_far = to(dx_s.at[3], dx_core.at[0], core)
     dx_to_far = to(dx_s.at[2], dx_far, far)
@@ -947,6 +979,10 @@
         dv_s[...] = jnp.zeros_like(dv_s)
 
         def block_step(b, inner):
+            @pl.when(i == 1)
+            def _():
+                probabilities(row, b)
+
             attend(row, b)
             for when, tasks in schedule.items():
 
@@ -1003,7 +1039,7 @@
     grad_core.start()
     def begin_h():
         for d in range(2):
-            sums_ref[place, rows_f:, lanes(d)] = last_q(d).astype(BF16)
+            done_q[rows_at(place, rows_q), lanes(d)] = last_q(d).astype(BF16)
         start_h(0)
 
     later += [begin_h] + groups(step_h, 6)
@@ -1029,7 +1065,7 @@
 
 
 def backward_attention(
-    hidden, q, k, v, wq, wk, wv, seg, dctx, one, common, sum_a, sum_b, far_b,
+    hidden, q, k, v, logs, wq, wk, wv, seg, dctx, one, common, sum_a, sum_b, far_b,
     dp_count, rows_q
 ):
     tokens, width = q.shape
@@ -1043,15 +1079,19 @@
         backward_kernel,
         out_shape=[
             shape((tokens, D), BF16),
-            shape((dp_count, chunk_a + chunk_b + rows_q, D), BF16),
+            shape((rows_a, D), BF16),
+            shape((rows_b, D), BF16),
+            shape((dp_count * rows_q, D), BF16),
         ],
-        in_specs=[ANY] * 4 + [VMEM] * 4 + [ANY, ANY, VMEM] + [ANY] * 3,
-        out_specs=[ANY, VMEM],
+        in_specs=[ANY] * 5 + [VMEM] * 4 + [ANY, ANY, VMEM] + [ANY] * 3,
+        out_specs=[ANY, VMEM, VMEM, VMEM],
         scratch_shapes=[
             pltpu.VMEM((tokens, D), BF16),
             pltpu.VMEM((tokens, width), BF16),
             pltpu.VMEM((tokens, width), BF16),
             pltpu.VMEM((tokens, width), BF16),
+            pltpu.VMEM(logs.shape, F32),
+            pltpu.VMEM((LEN // BLOCK, logs.shape[2], LEN), BF16),
             pltpu.VMEM((own, D), F32),
             pltpu.VMEM((own, D), BF16),
             pltpu.VMEM((tokens, width), BF16),
@@ -1074,7 +1114,7 @@
             pltpu.VMEM((2, chunk_a, D), BF16),
             dma((21,)),
             dma((21,)),
-            dma((12,)),
+            dma((13,)),
         ]
         + [dma(steps)] * 14,
         compiler_params=pltpu.CompilerParams(
@@ -1084,11 +1124,114 @@
             flops=24 * 10**9, bytes_accessed=40 << 20, transcendentals=1 << 23
         ),
         name="backward_attention",
-    )(hidden, q, k, v, wq, wk, wv, seg, dctx, one, common, sum_a, sum_b, far_b)
+    )(hidden, q, k, v, logs, wq, wk, wv, seg, dctx, one, common, sum_a, sum_b, far_b)
 
 
 def padded(rows, dp_count):
     return -(-rows // (16 * dp_count)) * 16
+
+
+PIECE, WIDE = 64, 256
+
+
+def finish_kernel(
+    grad_in, out_in, inner_in, outer_in, late_in, proj_in, q_in, k_in, v_in, side_in, small_in,
+    grad_ref, out_ref, inner_ref, outer_ref, proj_ref, q_ref, k_ref, v_ref, bq_ref, bv_ref,
+    bi_ref, *common,
+):
+    step = pl.program_id(0)
+    width = bq_ref.shape[0]
+    grad_ref[...] = grad_in[...].astype(F32)
+    out_ref[...] = out_in[...]
+    inner_ref[...] = inner_in[...].astype(F32)
+    early = early_rows(bi_ref.shape[0]) // WIDE
+
+    @pl.when(step < early)
+    def _():
+        outer_ref[...] = outer_in[...].astype(F32)
+
+    @pl.when(step >= early)
+    def _():
+        outer_ref[...] = late_in[...].astype(F32)
+
+    proj_ref[...] = proj_in[...].astype(F32)
+    q_ref[...] = q_in[...].astype(F32)
+    k_ref[...] = k_in[...].astype(F32)
+    v_ref[...] = v_in[...].astype(F32)
+
+    @pl.when(step == 0)
+    def _():
+        side = side_in[...].astype(F32)
+        bi_ref[...] = side[0:1].reshape(-1)
+        small = small_in[...].astype(F32)
+        bq_ref[...] = small[0:1, :width].reshape(-1)
+        bv_ref[...] = small[1:2, :width].reshape(-1)
+        for n, ref in enumerate(common):
+            ref[...] = small[16 + n : 17 + n].reshape(-1)
+
+
+def finish(grad_low, layer_out, sums_a, sums_b, sums_q, units, width):
+    tokens = grad_low.shape[0]
+    grid = 4
+    part = tokens // grid
+    early = early_rows(units)
+    base = 2 * units - early
+    blocks, few = units // WIDE, width // PIECE
+    first_late = (units - early) // WIDE
+    shape = jax.ShapeDtypeStruct
+    rows = lambda at: pl.BlockSpec((PIECE, D), lambda s: (at(s), 0))
+    capped = lambda first, most: rows(lambda s: first // PIECE + jnp.minimum(s, most - 1))
+    wide = lambda at: pl.BlockSpec((WIDE, D), lambda s: (at(s), 0))
+    whole = lambda n: pl.BlockSpec((n,), lambda s: (0,))
+    return pl.pallas_call(
+        finish_kernel,
+        out_shape=[
+            shape((tokens, D), F32),
+            shape((tokens, D), BF16),
+            shape((units, D), F32),
+            shape((units, D), F32),
+            shape((width, D), F32),
+            shape((width, D), F32),
+            shape((width, D), F32),
+            shape((width, D), F32),
+            shape((width,), F32),
+            shape((width,), F32),
+            shape((units,), F32),
+        ]
+        + [shape((D,), F32)] * 6,
+        grid=(grid,),
+        in_specs=[
+            pl.BlockSpec((part, D), lambda s: (s, 0)),
+            pl.BlockSpec((part, D), lambda s: (s, 0)),
+            wide(lambda s: jnp.minimum(s, blocks - 1)),
+            wide(lambda s: jnp.minimum(s, early // WIDE - 1)),
+            wide(lambda s: jnp.clip(s, early // WIDE, blocks - 1) + first_late),
+            capped(base, few),
+            capped(0, few),
+            capped(width, few),
+            capped(2 * width, few),
+            pl.BlockSpec((PIECE, D), lambda s: ((base + width) // PIECE, 0)),
+            pl.BlockSpec((PIECE, D), lambda s: (3 * width // PIECE, 0)),
+        ],
+        out_specs=[
+            pl.BlockSpec((part, D), lambda s: (s, 0)),
+            pl.BlockSpec((part, D), lambda s: (s, 0)),
+            wide(lambda s: jnp.minimum(s, blocks - 1)),
+            wide(lambda s: jnp.minimum(s, blocks - 1)),
+            capped(0, few),
+            capped(0, few),
+            capped(0, few),
+            capped(0, few),
+            whole(width),
+            whole(width),
+            whole(units),
+        ]
+        + [whole(D)] * 6,
+        compiler_params=pltpu.CompilerParams(vmem_limit_bytes=63 << 20),
+        name="finish",
+    )(
+        grad_low, layer_out, sums_a, sums_b, sums_a, sums_a, sums_q, sums_q, sums_q, sums_a, sums_q
+    )
 
 
 def on_device(
@@ -1123,7 +1266,7 @@
     segment_rows = segment_ids.reshape(row_count, LEN)
     seg_row = segment_rows[:, None, :]
 
-    query_rows, key_rows, value_rows, ctx, wi_all, wo_all, wp_all, bi_all = forward_attention(
+    query_rows, key_rows, value_rows, logs, ctx, wi_all, wo_all, wp_all, bi_all = forward_attention(
         hidden,
         w_query.T,
         b_query.reshape(1, -1),
@@ -1155,36 +1298,17 @@
     )
 
     rows_q = padded(3 * width + 24, dp_count)
-    grad_low, sums = backward_attention(
-        hidden, query_rows, key_rows, value_rows, w_query.T, w_key.T, w_value.T, seg_row, dctx, grad_one,
+    grad_low, sums_a, sums_b, sums_q = backward_attention(
+        hidden, query_rows, key_rows, value_rows, logs, w_query.T, w_key.T, w_value.T, seg_row, dctx, grad_one,
         common, sum_a, sum_b, far_b, dp_count, rows_q,
     )
-    chunk_a, rows_f = rows_a // dp_count, (rows_a + rows_b) // dp_count
-    sums_a = sums[:, :chunk_a].reshape(-1, D)
-    sums_b = sums[:, chunk_a:rows_f].reshape(-1, D)
-    sums_q = sums[:, rows_f:].reshape(-1, D)
-    sums_p = sums_a[base : base + width + 1].astype(F32)
-    sums_o = jnp.concatenate([sums_b[:early], sums_a[units:base]], axis=0)
-    small = sums_q[3 * width :].astype(F32)
+    (
+        grad_hidden, layer_out, g_inner, g_outer, g_out, g_query, g_key, g_value, g_bq, g_bv, g_bi,
+        g_bo, g_gain_a, g_shift_a, g_bu, g_gain_f, g_shift_f,
+    ) = finish(grad_low, layer_out, sums_a, sums_b, sums_q, units, width)
     return (
-        mean_loss.reshape(1),
-        layer_out,
-        grad_low.astype(F32),
-        sums_q[:width].astype(F32).T,
-        small[0, :width],
-        sums_q[width : 2 * width].astype(F32).T,
-        sums_q[2 * width : 3 * width].astype(F32).T,
-        small[1, :width],
-        sums_p[:width],
-        small[16],
-        small[17],
-        small[18],
-        sums_a[:units].astype(F32),
-        sums_p[width],
-        sums_o.astype(F32),
-        small[19],
-        small[20],
-        small[21],
+        mean_loss.reshape(1), layer_out, grad_hidden, g_query.T, g_bq, g_key.T, g_value.T, g_bv,
+        g_out, g_bo, g_gain_a, g_shift_a, g_inner, g_bi, g_outer, g_bu, g_gain_f, g_shift_f,
     )
 
 

time: 237 us -> 233 us (0.983)
  Pallas kernels: 215 us -> 227 us
  local copies, waits for them, and re-layouts: 10 us -> 1.42 us
  other arithmetic: 8.48 us -> 1.37 us
    pallas_call x0 -> x1, Pallas kernels: none -> 10.3 us  [finish(): pl.pallas_call(finish_kernel, out_shape=[shape((tokens, D), F32), shape((...]
    slice x7 -> x0, local copies, waits for them, and re-layouts: 6.24 us -> none  [the longest x1 1.68 us: on_device(): sums_a = sums[:, :chunk_a].reshape(-1, D)]
    convert_element_type x4 -> x0, other arithmetic: 5.87 us -> none  [the longest x1 3.19 us: on_device(): grad_low.astype(F32)]
where the time goes in v1:
time: 233 us
  Pallas kernels  227 us (97%)
  between operations  2.54 us (1%)
    pallas_call x1, Pallas kernels, backward_attention(): pl.pallas_call(backward_kernel, out_shape=[shape((tokens, D), BF16), shap...  121 us
    pallas_call x1, Pallas kernels, middle(): pl.pallas_call(middle_kernel, out_shape=[shape(hidden.shape, BF16), shape...  52.6 us
    pallas_call x1, Pallas kernels, forward_attention(): pl.pallas_call(forward_kernel, out_shape=[shape((tokens, width), BF16)] *...  43.4 us
    pallas_call x1, Pallas kernels, finish(): pl.pallas_call(finish_kernel, out_shape=[shape((tokens, D), F32), shape((...  10.3 us

profile of v1, /device:TPU:0, one launch (start us, length us, event | category | flops | bytes accessed | tf_op | source)
XLA Modules:
  0.0 232.5 jit_solution(4345206528587815601)
XLA Ops:
  0.7 0.7 subtract_bitcast_fusion
  1.4 0.7 fusion
  2.0 0.1 reshape.65
  2.2 0.6 reshape.66.target_ref
  2.8 0.7 copy.39.spots_ref
  3.5 43.4 %forward_attention.1 = (bf16[2048,192]{1,0:T(8,128)(2,1)}, bf16[2048,192]{1,0:T(8,128)(2,1)}, bf16[2048,192]{1,0:T(8,128)(2,1)}, f32[2,8,384,1]{3,2,1,0:T(8,128)...) custom-call(bf16[2048,768]{1,0:T(8,128)(2,1)} %hidden_in.3, ...), custom_call_target="tpu_custom_call" | custom-call | flops 8000000000 | bytes 25165824 | tf_op jit(solution)/shard_map/forward_attention/pallas_call | solution.py:300
  46.9 52.6 %middle.1 = (bf16[2048,768]{1,0:T(8,128)(2,1)}, f32[512,768]{1,0:T(8,128)}, bf16[4,512,192]{2,1,0:T(8,128)(2,1)}, bf16[2,1280,768]{2,1,0:T(8,128)(2,1)}, bf16[51...) custom-call(bf16[4,512,192]{2,1,0:T(8,128)(2,1)} %get-tuple-element.56.ctx_in, ...), custom_call_target="tpu_custom_call" | custom-call | flops 17999998976 | bytes 41943040 | tf_op jit(solution)/shard_map/middle/pallas_call | solution.py:629
  99.5 120.8 %backward_attention.1 = (bf16[2048,768]{1,0:T(8,128)(2,1)}, bf16[1280,768]{1,0:T(8,128)(2,1)}, bf16[512,768]{1,0:T(8,128)(2,1)}, bf16[640,768]{1,0:T(8,128)(2,1)}) custom-call(bf16[2048,768]{1,0:T(8,128)(2,1)} %hidden_in.3, bf16[2048,192]{1,0:T(8,128)(2,1)} %get-tuple-element.62.q_in, bf16[2048,192]{1,0:T(8,128)(2,1)} %get-tuple-element.63.k_in, ...), custom_call_target="tpu_custom_call" | custom-call | flops 24000000000 | bytes 41943040 | tf_op jit(solution)/shard_map/backward_attention/pallas_call | solution.py:1078
  220.4 10.3 %finish.1 = (f32[2048,768]{1,0:T(8,128)}, bf16[2048,768]{1,0:T(8,128)(2,1)}, f32[768,768]{1,0:T(8,128)}, f32[768,768]{1,0:T(8,128)}, f32[192,768]{1,0:T(8,128)},...) custom-call(bf16[2048,768]{1,0:T(8,128)(2,1)} %get-tuple-element.72., ...), custom_call_target="tpu_custom_call" | custom-call | tf_op jit(solution)/shard_map/finish/pallas_call | solution.py:1186
  (2 shorter events, 0.0 us)

commit v2 on v1

--- a/solution.py
+++ b/solution.py
@@ -686,7 +686,8 @@
     )(ctx, wp, hidden, upstream, wi, wo, bi, *vectors, spots, targets)
 
 
-BACKWARD_TASKS = (0, 1, 3, 4, 6, 7, 8, 8, 9, 11, 12, 14, 15, 15)
+BACKWARD_TASKS = (1, 2, 4, 6, 7, 8, 9, 10, 11, 12, 13)
+EARLY_TASKS = (3, 5, 7)
 
 
 def ring_place(index, count):
@@ -941,8 +942,16 @@
     for copy in fetches[:3]:
         copy.wait()
 
+    early_tasks = [(when, todo.pop(0)) for when in EARLY_TASKS if todo]
+
     def early_block(b, carry):
         probabilities(first_row, b)
+        for when, act in early_tasks:
+
+            @pl.when(b == when)
+            def _(act=act):
+                act()
+
         return carry
 
     lax.fori_loop(0, LEN // BLOCK, early_block, 0)

time: 233 us -> 230 us (0.987)
    pallas_call x1, Pallas kernels: 121 us -> 118 us  [backward_attention(): pl.pallas_call(backward_kernel, out_shape=[shape((tokens, D), BF16), shap...]
where the time goes in v2:
time: 230 us
  Pallas kernels  225 us (98%)
  between operations  2.54 us (1%)
    pallas_call x1, Pallas kernels, backward_attention(): pl.pallas_call(backward_kernel, out_shape=[shape((tokens, D), BF16), shap...  118 us
    pallas_call x1, Pallas kernels, middle(): pl.pallas_call(middle_kernel, out_shape=[shape(hidden.shape, BF16), shape...  52.6 us
    pallas_call x1, Pallas kernels, forward_attention(): pl.pallas_call(forward_kernel, out_shape=[shape((tokens, width), BF16)] *...  43.4 us
    pallas_call x1, Pallas kernels, finish(): pl.pallas_call(finish_kernel, out_shape=[shape((tokens, D), F32), shape((...  10.3 us

profile of v2, /device:TPU:0, one launch (start us, length us, event | category | flops | bytes accessed | tf_op | source)
XLA Modules:
  0.0 230.1 jit_solution(4358066125828288674)
XLA Ops:
  0.7 0.7 subtract_bitcast_fusion
  1.4 0.7 fusion
  2.0 0.1 reshape.65
  2.2 0.6 reshape.66.target_ref
  2.8 0.7 copy.39.spots_ref
  3.5 43.4 %forward_attention.1 = (bf16[2048,192]{1,0:T(8,128)(2,1)}, bf16[2048,192]{1,0:T(8,128)(2,1)}, bf16[2048,192]{1,0:T(8,128)(2,1)}, f32[2,8,384,1]{3,2,1,0:T(8,128)...) custom-call(bf16[2048,768]{1,0:T(8,128)(2,1)} %hidden_in.3, ...), custom_call_target="tpu_custom_call" | custom-call | flops 8000000000 | bytes 25165824 | tf_op jit(solution)/shard_map/forward_attention/pallas_call | solution.py:300
  46.9 52.6 %middle.1 = (bf16[2048,768]{1,0:T(8,128)(2,1)}, f32[512,768]{1,0:T(8,128)}, bf16[4,512,192]{2,1,0:T(8,128)(2,1)}, bf16[2,1280,768]{2,1,0:T(8,128)(2,1)}, bf16[51...) custom-call(bf16[4,512,192]{2,1,0:T(8,128)(2,1)} %get-tuple-element.56.ctx_in, ...), custom_call_target="tpu_custom_call" | custom-call | flops 17999998976 | bytes 41943040 | tf_op jit(solution)/shard_map/middle/pallas_call | solution.py:629
  99.5 118.4 %backward_attention.1 = (bf16[2048,768]{1,0:T(8,128)(2,1)}, bf16[1280,768]{1,0:T(8,128)(2,1)}, bf16[512,768]{1,0:T(8,128)(2,1)}, bf16[640,768]{1,0:T(8,128)(2,1)}) custom-call(bf16[2048,768]{1,0:T(8,128)(2,1)} %hidden_in.3, bf16[2048,192]{1,0:T(8,128)(2,1)} %get-tuple-element.62.q_in, bf16[2048,192]{1,0:T(8,128)(2,1)} %get-tuple-element.63.k_in, ...), custom_call_target="tpu_custom_call" | custom-call | flops 24000000000 | bytes 41943040 | tf_op jit(solution)/shard_map/backward_attention/pallas_call | solution.py:1087
  217.9 10.3 %finish.1 = (f32[2048,768]{1,0:T(8,128)}, bf16[2048,768]{1,0:T(8,128)(2,1)}, f32[768,768]{1,0:T(8,128)}, f32[768,768]{1,0:T(8,128)}, f32[192,768]{1,0:T(8,128)},...) custom-call(bf16[2048,768]{1,0:T(8,128)(2,1)} %get-tuple-element.72., ...), custom_call_target="tpu_custom_call" | custom-call | tf_op jit(solution)/shard_map/finish/pallas_call | solution.py:1195
  (2 shorter events, 0.0 us)
